TPU v7x, 32 devices: a whole 2x2x4 slice. The times are simulated.
32 devices in a mesh: expert: 8 (over y, x, core), dp: 4 (over z).
Axes of the slice: x: 2, y: 2, z: 4, core: 2. Of those that a mesh axis runs over, the one named last changes fastest.
Arguments:
- tokens: bfloat16 [4096, 2048], P(('expert', 'dp')), may hold values from -6 to 6
- expert_ids: int32 [4096, 4], P(('expert', 'dp')), may hold values from 0 to 15, all different within a row; in each aligned block of 128 rows (0 to 127, 128 to 255, ...) at most 96 rows name the same one
- gate_probs: float32 [4096, 4], P(('expert', 'dp')), may hold values from 0.05 to 0.5
- expert_weights: bfloat16 [2048, 3, 16, 384], P(None, None, 'expert'), may hold values from -0.125 to 0.125
- out_grad: bfloat16 [4096, 2048], P(('expert', 'dp')), may hold values from -1.5 to 1.5
Outputs:
- layer_out: bfloat16 [4096, 2048], P(('expert', 'dp'))
- token_grad: bfloat16 [4096, 2048], P(('expert', 'dp'))
- gate_grad: float32 [4096, 4], P(('expert', 'dp'))
- weight_grad: float32 [2048, 3, 16, 384], P('dp', None, 'expert')
Inputs may be any that keep to these rules, and one draw needn't show every extreme that they name: `expert_ids`: each row names 4 different experts. Among the 128 rows of one device (aligned blocks of rows), no expert is named by more than 96 rows, and in some block some expert is named by exactly 96 rows.
All inputs are finite; a program needn't handle non-finite values.
Results may differ from a plain program's by a relative error of at most 0.0085.
Values may be sent and summed in bfloat16 or wider, within the bound.
A program may use at most 128 MiB of HBM per device.

v0:
```python
import jax
import jax.numpy as jnp
from jax import lax
from jax.sharding import PartitionSpec as P

F32 = jnp.float32
BF16 = jnp.bfloat16


def dot(a, b, ca, cb):
    return lax.dot_general(a, b, (((ca,), (cb,)), ((), ())), preferred_element_type=F32)


def local(tokens, expert_ids, gate_probs, expert_weights, out_grad):
    tok_count, top_count = expert_ids.shape
    d = tokens.shape[1]
    ranks = lax.axis_size("expert")
    me = lax.axis_index("expert")
    local_experts, h = expert_weights.shape[2:]
    n = ranks * tok_count
    eh = local_experts * h
    x = lax.all_gather(tokens, "expert", axis=0, tiled=True)
    small = jnp.concatenate([expert_ids.astype(F32), gate_probs], axis=1)
    small = lax.all_gather(small, "expert", axis=0, tiled=True)
    g = lax.all_gather(out_grad, "expert", axis=0, tiled=True)
    ids = small[:, :top_count].astype(jnp.int32)
    probs = small[:, top_count:]
    mine = me * local_experts + jnp.arange(local_experts, dtype=jnp.int32)
    hit = ids[:, :, None] == mine[None, None, :]
    p = jnp.sum(jnp.where(hit, probs[:, :, None], 0.0), axis=1)
    w = expert_weights.reshape(d, 3 * eh)
    wgu = w[:, : 2 * eh]
    wd = w[:, 2 * eh :]
    a = dot(x, wgu, 1, 0)
    gate = a[:, :eh].reshape(n, local_experts, h)
    up = a[:, eh:].reshape(n, local_experts, h)
    s = jax.nn.sigmoid(gate)
    hidden = gate * s * up
    ph = (p[:, :, None] * hidden).astype(BF16).reshape(n, eh)
    lpart = dot(ph, wd, 1, 1).astype(BF16)
    layer_out = lax.psum_scatter(lpart, "expert", scatter_dimension=0, tiled=True)
    wd_grad = dot(g, ph, 0, 0).astype(BF16)
    wd_grad = lax.psum_scatter(wd_grad, "dp", scatter_dimension=0, tiled=True)
    u = dot(g, wd, 1, 0).reshape(n, local_experts, h)
    gg = jnp.sum(u * hidden, axis=-1)
    hc = p[:, :, None] * u
    gc = (hc * up * s * (1.0 + gate * (1.0 - s))).astype(BF16).reshape(n, eh)
    uc = (hc * gate * s).astype(BF16).reshape(n, eh)
    cots = jnp.concatenate([gc, uc], axis=1)
    tpart = dot(cots, wgu, 1, 1).astype(BF16)
    token_grad = lax.psum_scatter(tpart, "expert", scatter_dimension=0, tiled=True)
    ggk = jnp.sum(jnp.where(hit, gg[:, None, :], 0.0), axis=2)
    gate_grad = lax.psum_scatter(ggk, "expert", scatter_dimension=0, tiled=True)
    wgu_grad = dot(x, cots, 0, 0).astype(BF16)
    wgu_grad = lax.psum_scatter(wgu_grad, "dp", scatter_dimension=0, tiled=True)
    wg = jnp.concatenate([wgu_grad, wd_grad], axis=1)
    weight_grad = wg.astype(F32).reshape(-1, 3, local_experts, h)
    return (layer_out, token_grad, gate_grad, weight_grad)


def solution(mesh):
    tok = P(("expert", "dp"), None)
    wsp = P(None, None, "expert", None)
    return jax.shard_map(
        local,
        mesh=mesh,
        in_specs=(tok, tok, tok, wsp, tok),
        out_specs=(tok, tok, tok, P("dp", None, "expert", None)),
        check_vma=False,
    )
```

profile of v0, /device:TPU:0, one launch (start us, length us, event | category | flops | bytes accessed | tf_op | source)
XLA Modules:
  0.0 438.3 jit_solution(9271335342334902050)
XLA Ops:
  7.2 0.0 all-gather.3.cloned.1.call-start
  7.2 0.7 all-gather.3.cloned.1.call-update
  7.9 0.0 all-gather.5.cloned.1.call-start
  7.9 0.7 all-gather.5.cloned.1.call-update
  8.6 0.0 reduce-scatter.16.cloned.1.call-start
  8.7 0.0 copy-start.6
  8.7 0.0 copy-start.7
  8.7 20.9 %reshape.38 = bf16[2048,2304]{1,0:T(8,128)(2,1)} reshape(bf16[2048,3,2,384]{3,2,1,0:T(2,128)(2,1)} %param.8) | data formatting | bytes 18874368 | tf_op jit(solution)/shard_map/reshape | solution.py:31
  29.6 0.0 copy-done.6
  29.6 0.0 copy-done.7
  29.6 10.5 %all_gather.9 = f32[1024,8]{0,1:T(8,128)S(1)} all-gather(f32[128,8]{0,1:T(8,128)S(1)} %pad_maximum_fusion.4), channel_id=1, replica_groups=mesh['expert'=8,'dp'=4] {'expert'}, dimensions={0}, use_global_device_ids=true | all-gather | bytes 36864 | tf_op jit(solution)/shard_map/all_gather | solution.py:24
  40.1 9.2 %all-gather.3.cloned.1.call-done = bf16[1024,2048]{1,0:T(8,128)(2,1)} async-done(((bf16[128,2048]{1,0:T(8,128)(2,1)}), bf16[1024,2048]{1,0:T(8,128)(2,1)}) %all-gather.3.cloned.1.call-update) | async-done | bytes 4194320 | tf_op jit(solution)/shard_map/all_gather | solution.py:22
  49.4 10.0 %fusion.3 = f32[1024,1536]{1,0:T(8,128)S(1)} fusion(bf16[1024,2048]{1,0:T(8,128)(2,1)} %all-gather.3.cloned.1.call-done, bf16[2048,2304]{1,0:T(8,128)(2,1)} %reshape.38), kind=kOutput, calls=%fused_computation.4 | convolution fusion | flops 6442450944 | bytes 16777216 | tf_op jit(solution)/shard_map/dot_general | solution.py:11
  59.4 0.0 copy-start
  59.4 3.5 fusion.16
  62.9 1.6 copy-done
  64.5 2.4 copy.35
  66.9 2.5 copy.37
  69.3 2.4 copy.38
  71.7 2.4 copy.39
  74.1 13.9 %all-gather.5.cloned.1.call-done = bf16[1024,2048]{1,0:T(8,128)(2,1)} async-done(((bf16[128,2048]{1,0:T(8,128)(2,1)}), bf16[1024,2048]{1,0:T(8,128)(2,1)}) %all-gather.5.cloned.1.call-update) | async-done | bytes 4194320 | tf_op jit(solution)/shard_map/all_gather | solution.py:25
  88.0 6.3 %fusion.9 = f32[1024,768]{0,1:T(8,128)S(1)} fusion(bf16[1024,2048]{1,0:T(8,128)(2,1)} %all-gather.5.cloned.1.call-done, bf16[2048,2304]{1,0:T(8,128)(2,1)} %reshape.38), kind=kOutput, calls=%fused_computation.16 | convolution fusion | flops 3221225472 | bytes 10485760 | tf_op jit(solution)/shard_map/dot_general | solution.py:11
  94.3 2.4 copy.34
  96.7 2.4 copy.40
  99.1 4.8 %multiply_reduce_fusion = f32[1024,2]{0,1:T(2,128)S(1)} fusion(f32[1024,2,384]{2,0,1:T(8,128)} %copy.40, f32[1024,2,384]{2,0,1:T(8,128)} %copy.39, f32[1024,2,384]{2,0,1:T(8,128)} %copy.37), kind=kLoop, calls=%fused_computation.10 | loop fusion | flops 5502976 | bytes 9445376 | tf_op jit(solution)/shard_map/reduce_sum | solution.py:45
  103.9 0.1 fusion.13
  104.0 0.2 copy.33
  104.2 2.4 mul.62
  106.7 0.0 copy-start.1
  106.7 1.9 copy.47
  108.5 1.1 copy.44
  109.6 0.0 reduce-scatter.16.cloned.1.call-update
  109.6 0.2 reduce-scatter.14.cloned.1.call-start
  109.9 0.0 copy-done.1
  109.9 0.0 copy-start.8
  109.9 6.0 %multiply_convert_fusion.1 = (bf16[1024,768]{1,0:T(8,128)(2,1)}, bf16[1024,768]{1,0:T(8,128)(2,1)}, bf16[1024,768]{1,0:T(8,128)(2,1)S(1)}) fusion(f32[1024,768]{1,0:T(8,128)} %bitcast.22, f32[1024,768]{1,0:T(8,128)S(1)} %copy-done.1, f32[1024,1536]{1,0:T(8,128)} %copy-done), kind=kLoop, calls=%fused_computation.12 | loop fusion | flops 14155776 | bytes 17301504 | tf_op jit(solution)/shard_map/convert_element_type | solution.py:47
  115.9 0.0 copy-start.2
  115.9 1.1 copy-done.2
  117.1 0.0 copy-done.8
  117.1 4.8 %fusion.8 = bf16[2048,768]{0,1:T(8,128)(2,1)} fusion(bf16[1024,768]{1,0:T(8,128)(2,1)S(1)} %get-tuple-element.32, bf16[1024,2048]{1,0:T(8,128)(2,1)S(1)} %copy-done.8), kind=kOutput, calls=%fused_computation.15 | convolution fusion | flops 3222798336 | bytes 8912896 | tf_op jit(solution)/shard_map/dot_general | solution.py:11
  121.9 0.0 copy-start.4
  121.9 0.0 copy-start.5
  121.9 0.0 reduce-scatter.14.cloned.1.call-update
  121.9 0.0 reduce-scatter.12.cloned.1.call-start
  122.0 1.3 copy-done.4
  123.3 0.5 copy-done.5
  123.8 10.9 %fusion = bf16[2048,1536]{0,1:T(8,128)(2,1)} fusion(bf16[1024,2048]{1,0:T(8,128)(2,1)} %all-gather.3.cloned.1.call-done, bf16[1024,768]{1,0:T(8,128)(2,1)S(1)} %copy-done.5, bf16[1024,768]{1,0:T(8,128)(2,1)S(1)} %copy-done.4), kind=kOutput, calls=%fused_computation.1 | convolution fusion | flops 6451888128 | bytes 13631488 | tf_op jit(solution)/shard_map/dot_general | solution.py:11
  134.7 0.0 reduce-scatter.12.cloned.1.call-update
  134.7 0.0 reduce-scatter.10.cloned.1.call-start
  134.8 11.0 %fusion.5 = bf16[1024,2048]{1,0:T(8,128)(2,1)} fusion(bf16[2048,2304]{1,0:T(8,128)(2,1)} %reshape.38, bf16[1024,768]{1,0:T(8,128)(2,1)S(1)} %copy-done.5, bf16[1024,768]{1,0:T(8,128)(2,1)S(1)} %copy-done.4), kind=kOutput, calls=%fused_computation.6 | convolution fusion | flops 6450839552 | bytes 13631488 | tf_op jit(solution)/shard_map/dot_general | solution.py:11
  145.8 0.0 copy-start.3
  145.8 0.0 reduce-scatter.10.cloned.1.call-update
  145.8 0.0 reduce-scatter.8.cloned.1.call-start
  145.8 1.3 copy-done.3
  147.2 6.9 %convolution_convert_fusion.1 = bf16[1024,2048]{1,0:T(8,128)(2,1)} fusion(bf16[1024,768]{1,0:T(8,128)(2,1)S(1)} %copy-done.3, bf16[2048,2304]{1,0:T(8,128)(2,1)} %reshape.38), kind=kOutput, calls=%fused_computation.7 | convolution fusion | flops 3223322624 | bytes 8912896 | tf_op jit(solution)/shard_map/dot_general | solution.py:11
  154.1 0.0 reduce-scatter.8.cloned.1.call-update
  154.1 0.0 reduce-scatter.16.cloned.1.call-done
  154.1 1.5 copy.45
  155.6 51.5 %reduce-scatter.14.cloned.1.call-done = bf16[512,768]{0,1:T(8,128)(2,1)} async-done(((bf16[2048,768]{0,1:T(8,128)(2,1)}), bf16[512,768]{0,1:T(8,128)(2,1)}) %reduce-scatter.14.cloned.1.call-update) | async-done | bytes 786448 | tf_op jit(solution)/shard_map/reduce_scatter | solution.py:43
  207.1 113.1 %reduce-scatter.12.cloned.1.call-done = bf16[512,1536]{0,1:T(8,128)(2,1)} async-done(((bf16[2048,1536]{0,1:T(8,128)(2,1)}), bf16[512,1536]{0,1:T(8,128)(2,1)}) %reduce-scatter.12.cloned.1.call-update) | async-done | bytes 1572880 | tf_op jit(solution)/shard_map/reduce_scatter | solution.py:55
  320.1 1.8 pad_maximum_fusion.1
  321.9 4.8 %copy.43 = f32[512,3,2,384]{3,2,1,0:T(2,128)} copy(bf16[512,3,2,384]{0,3,2,1:T(8,128)(2,1)S(1)} %bitcast.23) | data formatting | bytes 7077888
  326.7 49.5 %reduce-scatter.10.cloned.1.call-done = bf16[128,2048]{1,0:T(8,128)(2,1)} async-done(((bf16[1024,2048]{1,0:T(8,128)(2,1)}), bf16[128,2048]{1,0:T(8,128)(2,1)}) %reduce-scatter.10.cloned.1.call-update) | async-done | bytes 524304 | tf_op jit(solution)/shard_map/reduce_scatter | solution.py:51
  376.2 55.3 %reduce-scatter.8.cloned.1.call-done = bf16[128,2048]{1,0:T(8,128)(2,1)} async-done(((bf16[1024,2048]{1,0:T(8,128)(2,1)}), bf16[128,2048]{1,0:T(8,128)(2,1)}) %reduce-scatter.8.cloned.1.call-update) | async-done | bytes 524304 | tf_op jit(solution)/shard_map/reduce_scatter | solution.py:41
  (4 shorter events, 0.0 us)
Async XLA Ops:
  7.2 42.2 %all-gather.3.cloned.1.call-start = ((), (), s32[]{:S(2)}) async-start(), calls=%async_computation.5 | async-start | bytes 4718592 | tf_op jit(solution)/shard_map/all_gather | solution.py:22
  7.9 80.1 %all-gather.5.cloned.1.call-start = ((), (), s32[]{:S(2)}) async-start(), calls=%async_computation.7 | async-start | bytes 4718592 | tf_op jit(solution)/shard_map/all_gather | solution.py:25
  8.6 145.5 %reduce-scatter.16.cloned.1.call-start = ((), (), s32[]{:S(2)}) async-start(), calls=%async_computation.11 | async-start | bytes 589824
  8.7 20.9 %copy-start.6 = (s32[128,4]{0,1:T(4,128)S(1)}, s32[128,4]{0,1:T(4,128)}, u32[]{:S(2)}) copy-start(s32[128,4]{0,1:T(4,128)} %param.6) | copy-start | bytes 6148
  8.7 20.9 %copy-start.7 = (f32[128,4]{0,1:T(4,128)S(1)}, f32[128,4]{0,1:T(4,128)}, u32[]{:S(2)}) copy-start(f32[128,4]{0,1:T(4,128)} %param.7) | copy-start | bytes 6148
  59.4 5.1 %copy-start = (f32[1024,1536]{1,0:T(8,128)}, f32[1024,1536]{1,0:T(8,128)S(1)}, u32[]{:S(2)}) copy-start(f32[1024,1536]{1,0:T(8,128)S(1)} %fusion.3) | copy-start | bytes 18874372
  106.7 3.2 copy-start.1
  109.6 97.4 %reduce-scatter.14.cloned.1.call-start = ((), (), s32[]{:S(2)}) async-start(), calls=%async_computation.10 | async-start | bytes 3932160 | tf_op jit(solution)/shard_map/reduce_scatter | solution.py:43
  109.9 7.2 %copy-start.8 = (bf16[1024,2048]{1,0:T(8,128)(2,1)S(1)}, bf16[1024,2048]{1,0:T(8,128)(2,1)}, u32[]{:S(2)}) copy-start(bf16[1024,2048]{1,0:T(8,128)(2,1)} %all-gather.5.cloned.1.call-done) | copy-start | bytes 12582916
  115.9 1.1 copy-start.2
  121.9 1.4 copy-start.4
  121.9 1.9 copy-start.5
  121.9 198.2 %reduce-scatter.12.cloned.1.call-start = ((), (), s32[]{:S(2)}) async-start(), calls=%async_computation.9 | async-start | bytes 7864320 | tf_op jit(solution)/shard_map/reduce_scatter | solution.py:55
  134.7 241.5 %reduce-scatter.10.cloned.1.call-start = ((), (), s32[]{:S(2)}) async-start(), calls=%async_computation.8 | async-start | bytes 4718592 | tf_op jit(solution)/shard_map/reduce_scatter | solution.py:51
  145.8 1.4 copy-start.3
  145.8 285.7 %reduce-scatter.8.cloned.1.call-start = ((), (), s32[]{:S(2)}) async-start(), calls=%async_computation.6 | async-start | bytes 4718592 | tf_op jit(solution)/shard_map/reduce_scatter | solution.py:41
Sparse Core Ops, SparseCore 0:
  9.9 39.4 all-gather.2
  51.3 36.6 all-gather.4
  109.8 34.1 reduce-scatter.15
  146.8 60.2 reduce-scatter.13
  209.3 110.7 reduce-scatter.11
  324.3 51.8 reduce-scatter.9
  380.1 51.3 reduce-scatter.7
where the time goes:
time: 439 us; the launch traced here: 438 us
  waiting for transfers between devices  294 us (67%)
  local copies, waits for them, and re-layouts  56.4 us (13%)
  matrix products  49.9 us (11%)
  between operations  14.3 us (3%)
  other arithmetic  12.8 us (3%)
  blocking collectives  10.5 us (2%)
    reduce_scatter x1, waiting for transfers between devices, local(): wgu_grad = lax.psum_scatter(wgu_grad, 'dp', scatter_dimension=0, tiled=True)  113 us
    reduce_scatter x1, waiting for transfers between devices, local(): lax.psum_scatter(lpart, 'expert', scatter_dimension=0, tiled=True)  55.3 us
    reduce_scatter x1, waiting for transfers between devices, local(): wd_grad = lax.psum_scatter(wd_grad, 'dp', scatter_dimension=0, tiled=True)  51.5 us
    dot_general x6, matrix products, dot(): lax.dot_general(a, b, (((ca,), (cb,)), ((), ())), preferred_element_type=...  49.9 us
    reduce_scatter x1, waiting for transfers between devices, local(): lax.psum_scatter(tpart, 'expert', scatter_dimension=0, tiled=True)  49.5 us
    reshape x1, local copies, waits for them, and re-layouts, local(): w = expert_weights.reshape(d, 3 * eh)  20.9 us
    unnamed x22, local copies, waits for them, and re-layouts  15.1 us
    all_gather x1, waiting for transfers between devices, local(): g = lax.all_gather(out_grad, 'expert', axis=0, tiled=True)  13.9 us
  transfers between devices with their start and end apart: 7, of which 6 were waited for; matrix products, arithmetic and copies ran while one was open for 21% of the time, Pallas kernels for 0%

commit v1 on v0

--- a/solution.py
+++ b/solution.py
@@ -5,6 +5,11 @@
 
 F32 = jnp.float32
 BF16 = jnp.bfloat16
+press_region_now = lambda local_values, packet, comm_axis: jnp.split(
+    lax.all_gather(jnp.concatenate([local_values, packet], 1), comm_axis, axis=0, tiled=True),
+    [local_values.shape[1]],
+    1,
+)
 
 
 def dot(a, b, ca, cb):
@@ -19,9 +24,8 @@
     local_experts, h = expert_weights.shape[2:]
     n = ranks * tok_count
     eh = local_experts * h
-    x = lax.all_gather(tokens, "expert", axis=0, tiled=True)
     small = jnp.concatenate([expert_ids.astype(F32), gate_probs], axis=1)
-    small = lax.all_gather(small, "expert", axis=0, tiled=True)
+    x, small = press_region_now(tokens, small, "expert")
     g = lax.all_gather(out_grad, "expert", axis=0, tiled=True)
     ids = small[:, :top_count].astype(jnp.int32)
     probs = small[:, top_count:]

time: 439 us -> 474 us (1.080)
  waiting for transfers between devices: 294 us -> 327 us
  blocking collectives: 10.5 us -> 0 us
  local copies, waits for them, and re-layouts: 56.4 us -> 62 us
    all_gather x1, waiting for transfers between devices: 9.23 us -> 46.9 us  [lax.all_gather(jnp.concatenate([local_values, packet], 1), comm_axis, axi...]
    all_gather x1 -> x0, blocking collectives: 10.5 us -> none  [local(): small = lax.all_gather(small, 'expert', axis=0, tiled=True)]
    convert_element_type x0 -> x1, local copies, waits for them, and re-layouts: none -> 6.45 us  [local(): weight_grad = wg.astype(F32).reshape(-1, 3, local_experts, h)]
    unnamed x22 -> x18, local copies, waits for them, and re-layouts: 15.1 us -> 11.4 us
  transfers between devices with their start and end apart: 7 -> 7, of which waited for: 6 -> 6; matrix products, arithmetic and copies ran while one was open for 21% -> 19% of each run, Pallas kernels for 0% -> 0%
where the time goes in v1:
time: 474 us; the launch traced here: 473 us
  waiting for transfers between devices  327 us (69%)
  local copies, waits for them, and re-layouts  62 us (13%)
  matrix products  52.7 us (11%)
  other arithmetic  16.6 us (4%)
  between operations  14.2 us (3%)
    reduce_scatter x1, waiting for transfers between devices, local(): wgu_grad = lax.psum_scatter(wgu_grad, 'dp', scatter_dimension=0, tiled=True)  113 us
    reduce_scatter x1, waiting for transfers between devices, local(): lax.psum_scatter(lpart, 'expert', scatter_dimension=0, tiled=True)  55.3 us
    dot_general x6, matrix products, dot(): lax.dot_general(a, b, (((ca,), (cb,)), ((), ())), preferred_element_type=...  52.7 us
    reduce_scatter x1, waiting for transfers between devices, local(): wd_grad = lax.psum_scatter(wd_grad, 'dp', scatter_dimension=0, tiled=True)  49.9 us
    all_gather x1, waiting for transfers between devices, lax.all_gather(jnp.concatenate([local_values, packet], 1), comm_axis, axi...  46.9 us
    reduce_scatter x1, waiting for transfers between devices, local(): lax.psum_scatter(tpart, 'expert', scatter_dimension=0, tiled=True)  45.5 us
    reshape x1, local copies, waits for them, and re-layouts, local(): w = expert_weights.reshape(d, 3 * eh)  20.9 us
    all_gather x1, waiting for transfers between devices, local(): g = lax.all_gather(out_grad, 'expert', axis=0, tiled=True)  15.5 us
  transfers between devices with their start and end apart: 7, of which 6 were waited for; matrix products, arithmetic and copies ran while one was open for 19% of the time, Pallas kernels for 0%

profile of v1, /device:TPU:0, one launch (start us, length us, event | category | flops | bytes accessed | tf_op | source)
XLA Modules:
  0.0 473.0 jit_solution(226390186206413161)
XLA Ops:
  7.2 0.0 all-gather.5.cloned.1.call-start
  7.2 0.7 all-gather.5.cloned.1.call-update
  7.9 0.0 all-gather.3.cloned.1.call-start
  7.9 1.3 copy.42
  9.3 0.7 convert_element_type.44
  9.9 2.9 concatenate.9
  12.8 0.0 all-gather.3.cloned.1.call-update
  12.9 0.0 reduce-scatter.16.cloned.1.call-start
  12.9 20.9 %reshape.38 = bf16[2048,2304]{1,0:T(8,128)(2,1)} reshape(bf16[2048,3,2,384]{3,2,1,0:T(2,128)(2,1)} %param.8) | data formatting | bytes 18874368 | tf_op jit(solution)/shard_map/reshape | solution.py:35
  33.8 15.5 %all-gather.5.cloned.1.call-done = bf16[1024,2048]{1,0:T(8,128)(2,1)} async-done(((bf16[128,2048]{1,0:T(8,128)(2,1)}), bf16[1024,2048]{1,0:T(8,128)(2,1)}) %all-gather.5.cloned.1.call-update) | async-done | bytes 4194320 | tf_op jit(solution)/shard_map/all_gather | solution.py:29
  49.3 6.3 %fusion.14 = f32[1024,768]{0,1:T(8,128)S(1)} fusion(bf16[1024,2048]{1,0:T(8,128)(2,1)} %all-gather.5.cloned.1.call-done, bf16[2048,2304]{1,0:T(8,128)(2,1)} %reshape.38), kind=kOutput, calls=%fused_computation.18 | convolution fusion | flops 3221225472 | bytes 10485760 | tf_op jit(solution)/shard_map/dot_general | solution.py:16
  55.6 2.4 copy.44
  58.1 2.4 copy.50
  60.4 46.9 %all-gather.3.cloned.1.call-done = f32[1024,2056]{0,1:T(8,128)} async-done(((f32[128,2056]{0,1:T(8,128)}), f32[1024,2056]{0,1:T(8,128)}) %all-gather.3.cloned.1.call-update) | async-done | bytes 8421392 | tf_op jit(solution)/shard_map/all_gather | solution.py:9
  107.3 11.3 %fusion.2 = f32[1024,1536]{1,0:T(8,128)S(1)} fusion(f32[1024,2056]{0,1:T(8,128)} %all-gather.3.cloned.1.call-done, bf16[2048,2304]{1,0:T(8,128)(2,1)} %reshape.38), kind=kOutput, calls=%fused_computation.2 | convolution fusion | flops 6442450944 | bytes 16777216 | tf_op jit(solution)/shard_map/dot_general | solution.py:16
  118.6 0.0 copy-start
  118.6 3.4 fusion.22
  122.0 1.3 copy-done
  123.3 2.4 copy.45
  125.7 2.5 copy.47
  128.2 2.4 copy.48
  130.6 2.3 copy.49
  132.9 4.8 %multiply_reduce_fusion = f32[1024,2]{0,1:T(2,128)S(1)} fusion(f32[1024,2,384]{2,0,1:T(8,128)} %copy.50, f32[1024,2,384]{2,0,1:T(8,128)} %copy.49, f32[1024,2,384]{2,0,1:T(8,128)} %copy.47), kind=kLoop, calls=%fused_computation.12 | loop fusion | flops 5502976 | bytes 9445376 | tf_op jit(solution)/shard_map/reduce_sum | solution.py:49
  137.7 0.8 fusion.21
  138.6 0.1 fusion.18
  138.7 0.2 copy.43
  138.9 2.4 mul.62
  141.3 0.0 copy-start.1
  141.3 1.9 copy.58
  143.2 1.0 copy.55
  144.3 0.0 reduce-scatter.16.cloned.1.call-update
  144.3 0.2 reduce-scatter.14.cloned.1.call-start
  144.5 0.0 copy-done.1
  144.5 0.0 copy-start.6
  144.5 6.0 %multiply_convert_fusion.1 = (bf16[1024,768]{1,0:T(8,128)(2,1)}, bf16[1024,768]{1,0:T(8,128)(2,1)}, bf16[1024,768]{1,0:T(8,128)(2,1)S(1)}) fusion(f32[1024,768]{1,0:T(8,128)} %bitcast.16, f32[1024,768]{1,0:T(8,128)S(1)} %copy-done.1, f32[1024,1536]{1,0:T(8,128)} %copy-done), kind=kLoop, calls=%fused_computation.14 | loop fusion | flops 14155776 | bytes 17301504 | tf_op jit(solution)/shard_map/convert_element_type | solution.py:51
  150.5 0.0 copy-start.2
  150.6 1.2 copy-done.2
  151.8 0.0 copy-done.6
  151.8 5.0 %fusion.13 = bf16[2048,768]{1,0:T(8,128)(2,1)} fusion(bf16[1024,768]{1,0:T(8,128)(2,1)S(1)} %get-tuple-element.8, bf16[1024,2048]{1,0:T(8,128)(2,1)S(1)} %copy-done.6), kind=kOutput, calls=%fused_computation.17 | convolution fusion | flops 3222798336 | bytes 8912896 | tf_op jit(solution)/shard_map/dot_general | solution.py:16
  156.8 0.0 copy-start.4
  156.8 0.0 copy-start.5
  156.8 0.0 reduce-scatter.14.cloned.1.call-update
  156.8 0.0 reduce-scatter.12.cloned.1.call-start
  156.9 1.3 copy-done.4
  158.2 0.5 copy-done.5
  158.7 12.1 %fusion.4 = bf16[2048,1536]{1,0:T(8,128)(2,1)} fusion(f32[1024,2056]{0,1:T(8,128)} %all-gather.3.cloned.1.call-done, bf16[1024,768]{1,0:T(8,128)(2,1)S(1)} %copy-done.5, bf16[1024,768]{1,0:T(8,128)(2,1)S(1)} %copy-done.4), kind=kOutput, calls=%fused_computation.4 | convolution fusion | flops 6448742400 | bytes 13631488 | tf_op jit(solution)/shard_map/dot_general | solution.py:16
  170.8 0.0 reduce-scatter.12.cloned.1.call-update
  170.8 0.0 reduce-scatter.10.cloned.1.call-start
  170.9 11.1 %fusion.10 = bf16[1024,2048]{1,0:T(8,128)(2,1)} fusion(bf16[2048,2304]{1,0:T(8,128)(2,1)} %reshape.38, bf16[1024,768]{1,0:T(8,128)(2,1)S(1)} %copy-done.5, bf16[1024,768]{1,0:T(8,128)(2,1)S(1)} %copy-done.4), kind=kOutput, calls=%fused_computation.8 | convolution fusion | flops 6450839552 | bytes 13631488 | tf_op jit(solution)/shard_map/dot_general | solution.py:16
  182.0 0.0 copy-start.3
  182.0 0.0 reduce-scatter.10.cloned.1.call-update
  182.1 0.0 reduce-scatter.8.cloned.1.call-start
  182.1 1.3 copy-done.3
  183.4 6.8 %convolution_convert_fusion = bf16[1024,2048]{1,0:T(8,128)(2,1)} fusion(bf16[1024,768]{1,0:T(8,128)(2,1)S(1)} %copy-done.3, bf16[2048,2304]{1,0:T(8,128)(2,1)} %reshape.38), kind=kOutput, calls=%fused_computation.9 | convolution fusion | flops 3223322624 | bytes 8912896 | tf_op jit(solution)/shard_map/dot_general | solution.py:16
  190.3 0.0 reduce-scatter.8.cloned.1.call-update
  190.3 0.0 reduce-scatter.16.cloned.1.call-done
  190.3 1.5 copy.56
  191.8 49.9 %reduce-scatter.14.cloned.1.call-done = bf16[512,768]{1,0:T(8,128)(2,1)} async-done(((bf16[2048,768]{1,0:T(8,128)(2,1)}), bf16[512,768]{1,0:T(8,128)(2,1)}) %reduce-scatter.14.cloned.1.call-update) | async-done | bytes 786448 | tf_op jit(solution)/shard_map/reduce_scatter | solution.py:47
  241.7 113.1 %reduce-scatter.12.cloned.1.call-done = bf16[512,1536]{1,0:T(8,128)(2,1)} async-done(((bf16[2048,1536]{1,0:T(8,128)(2,1)}), bf16[512,1536]{1,0:T(8,128)(2,1)}) %reduce-scatter.12.cloned.1.call-update) | async-done | bytes 1572880 | tf_op jit(solution)/shard_map/reduce_scatter | solution.py:59
  354.8 4.1 maximum_convert_fusion
  358.9 6.4 %reshape.42 = f32[512,3,2,384]{3,2,1,0:T(2,128)} reshape(f32[512,2304]{1,0:T(8,128)} %maximum_convert_fusion) | data formatting | bytes 9437184 | tf_op jit(solution)/shard_map/convert_element_type | solution.py:61
  365.4 45.5 %reduce-scatter.10.cloned.1.call-done = bf16[128,2048]{1,0:T(8,128)(2,1)} async-done(((bf16[1024,2048]{1,0:T(8,128)(2,1)}), bf16[128,2048]{1,0:T(8,128)(2,1)}) %reduce-scatter.10.cloned.1.call-update) | async-done | bytes 524304 | tf_op jit(solution)/shard_map/reduce_scatter | solution.py:55
  410.8 55.3 %reduce-scatter.8.cloned.1.call-done = bf16[128,2048]{1,0:T(8,128)(2,1)} async-done(((bf16[1024,2048]{1,0:T(8,128)(2,1)}), bf16[128,2048]{1,0:T(8,128)(2,1)}) %reduce-scatter.8.cloned.1.call-update) | async-done | bytes 524304 | tf_op jit(solution)/shard_map/reduce_scatter | solution.py:45
  (1 shorter events, 0.0 us)
Async XLA Ops:
  7.2 42.2 %all-gather.5.cloned.1.call-start = ((), (), s32[]{:S(2)}) async-start(), calls=%async_computation.7 | async-start | bytes 4718592 | tf_op jit(solution)/shard_map/all_gather | solution.py:29
  7.9 99.4 %all-gather.3.cloned.1.call-start = ((), (), s32[]{:S(2)}) async-start(), calls=%async_computation.5 | async-start | bytes 9474048 | tf_op jit(solution)/shard_map/all_gather | solution.py:9
  12.9 177.5 %reduce-scatter.16.cloned.1.call-start = ((), (), s32[]{:S(2)}) async-start(), calls=%async_computation.11 | async-start | bytes 589824
  118.6 4.7 copy-start
  141.3 3.2 copy-start.1
  144.3 97.4 %reduce-scatter.14.cloned.1.call-start = ((), (), s32[]{:S(2)}) async-start(), calls=%async_computation.10 | async-start | bytes 3932160 | tf_op jit(solution)/shard_map/reduce_scatter | solution.py:47
  144.5 7.2 %copy-start.6 = (bf16[1024,2048]{1,0:T(8,128)(2,1)S(1)}, bf16[1024,2048]{1,0:T(8,128)(2,1)}, u32[]{:S(2)}) copy-start(bf16[1024,2048]{1,0:T(8,128)(2,1)} %all-gather.5.cloned.1.call-done) | copy-start | bytes 12582916
  150.5 1.2 copy-start.2
  156.8 1.4 copy-start.4
  156.8 1.9 copy-start.5
  156.8 198.0 %reduce-scatter.12.cloned.1.call-start = ((), (), s32[]{:S(2)}) async-start(), calls=%async_computation.9 | async-start | bytes 7864320 | tf_op jit(solution)/shard_map/reduce_scatter | solution.py:59
  170.8 240.0 %reduce-scatter.10.cloned.1.call-start = ((), (), s32[]{:S(2)}) async-start(), calls=%async_computation.8 | async-start | bytes 4718592 | tf_op jit(solution)/shard_map/reduce_scatter | solution.py:55
  182.0 1.4 copy-start.3
  182.1 284.1 %reduce-scatter.8.cloned.1.call-start = ((), (), s32[]{:S(2)}) async-start(), calls=%async_computation.6 | async-start | bytes 4718592 | tf_op jit(solution)/shard_map/reduce_scatter | solution.py:45
Sparse Core Ops, SparseCore 0:
  9.9 39.4 all-gather.4
  51.2 56.0 all-gather.2
  144.4 34.1 reduce-scatter.15
  181.4 60.2 reduce-scatter.13
  244.0 110.7 reduce-scatter.11
  359.0 51.8 reduce-scatter.9
  414.8 51.2 reduce-scatter.7
